TPU v7x, 256 devices: a whole 4x4x8 slice. The times are simulated.
256 devices in a mesh: body: 8 (over z), gx: 8 (over y, core), gy: 4 (over x).
Axes of the slice: x: 4, y: 4, z: 8, core: 2. Of those that a mesh axis runs over, the one named last changes fastest.
Arguments:
- load: float32 [128, 512, 512], P('body', 'gx', 'gy'), may hold values from -8 to 8
- stiffness: float32 [128, 512, 512], P('body', 'gx', 'gy'), may hold values from 0.1 to 3
- pair_code: int32 [4, 512, 512], P(None, 'gx', 'gy'), may hold values from 0 to 24
- pair_weight: float32 [4, 512, 512], P(None, 'gx', 'gy'), may hold values from 0.05 to 0.5
Outputs:
- solution: float32 [128, 512, 512], P('body', 'gx', 'gy')
- interface_load: float32 [128, 512, 512], P('body', 'gx', 'gy')
Inputs may be any that keep to these rules, and one draw needn't show every extreme that they name: `pair_code`: entry k of slave node (i, j) ties it to the master node (i + c // 5 - 2, j + c % 5 - 2) of the top layer of the body below, c being the entry; the same pairing holds at every interface; masters outside the grid count as zero.
All inputs are finite; a program needn't handle non-finite values.
Results may differ from a plain program's by a relative error of at most 0.0001.
Values sent between devices are 32-bit elements; how exact they have to be, the bound alone decides.
A program may use at most 64 MiB of HBM per device.

v0:
```python
import jax
import jax.numpy as jnp
from jax import lax
from jax.sharding import PartitionSpec as P

REACH = 2
UZAWA = 2
INNER = 3


RATE = 2.0


def with_halo(cells, sides, width):
    for axis, dim in sides:
        count = lax.axis_size(axis)
        ends = count - 1
        head = lax.slice_in_dim(cells, 0, width, axis=dim)
        tail = lax.slice_in_dim(cells, cells.shape[dim] - width, cells.shape[dim], axis=dim)
        cells = jnp.concatenate(
            [
                lax.ppermute(tail, axis, [(i, (i + 1) % count) for i in range(ends)]),
                cells,
                lax.ppermute(head, axis, [((i + 1) % count, i) for i in range(ends)]),
            ],
            axis=dim,
        )
    return cells


def sent_to_all(array, axis):
    copies = jnp.broadcast_to(array, (lax.axis_size(axis), *array.shape))
    return lax.all_to_all(copies, axis, split_axis=0, concat_axis=0, tiled=True)


def taken_together(array, axis):
    return sent_to_all(array, axis).sum(axis=0)


def in_one(arrays, axis):
    vector, at, finished = (jnp.concatenate([a.reshape(-1) for a in arrays]), 0, [])
    running = taken_together(vector, axis)
    for a in arrays:
        finished.append(running[at : at + a.size].reshape(a.shape))
        at += a.size
    return tuple(finished)


def passed_along(array, axis, by):
    count = lax.axis_size(axis)
    pairs = [(i, i + by) for i in range(count) if 0 <= i + by < count]
    return lax.ppermute(array, axis, pairs)


def build_tables(codes, weights):
    offset_span = 2 * REACH + 1
    tables = []
    for offset in range(offset_span * offset_span):
        tables.append(jnp.sum(jnp.where(codes == offset, weights, 0.0), axis=0))
    return jnp.stack(tables)


def pull_sum(tables, source, face_rows, face_cols):
    offset_span = 2 * REACH + 1
    pulled = jnp.zeros((face_rows, face_cols), jnp.float32)
    for offset in range(offset_span * offset_span):
        shift_row = offset // offset_span - REACH
        shift_col = offset % offset_span - REACH
        window = source[
            REACH + shift_row : REACH + shift_row + face_rows,
            REACH + shift_col : REACH + shift_col + face_cols,
        ]
        pulled = pulled + tables[offset] * window
    return pulled


def push_sum(tables_grown, multiplier_grown, face_rows, face_cols):
    offset_span = 2 * REACH + 1
    force = jnp.zeros((face_rows, face_cols), jnp.float32)
    for offset in range(offset_span * offset_span):
        shift_row = offset // offset_span - REACH
        shift_col = offset % offset_span - REACH
        spread = tables_grown[offset] * multiplier_grown
        force = (
            force
            + spread[
                REACH - shift_row : REACH - shift_row + face_rows,
                REACH - shift_col : REACH - shift_col + face_cols,
            ]
        )
    return force


def per_device(load, stiffness, pair_code, pair_weight):
    layers = load.shape[0]
    face_rows = load.shape[1]
    face_cols = load.shape[2]
    position = lax.axis_index("body")
    has_above = position < lax.axis_size("body") - 1
    layer_index = lax.broadcasted_iota(jnp.int32, load.shape, 0)
    top_layer = layer_index == layers - 1
    bottom_layer = layer_index == 0

    def operate(vector):
        padded = with_halo(vector, (("gx", 1), ("gy", 2)), 1)
        stacked = jnp.pad(padded, ((1, 1), (0, 0), (0, 0)))
        beside = stacked[2:, 1:-1, 1:-1] + stacked[:-2, 1:-1, 1:-1]
        beside = beside + padded[:, 2:, 1:-1] + padded[:, :-2, 1:-1]
        beside = beside + padded[:, 1:-1, 2:] + padded[:, 1:-1, :-2]
        return (6.0 + stiffness) * vector - beside

    def two_products(residual, image):
        return in_one((jnp.sum(residual * residual), jnp.sum(residual * image)), ("gx", "gy"))

    grown_rows = face_rows + 2 * REACH
    grown_cols = face_cols + 2 * REACH
    codes_grown = with_halo(pair_code, (("gx", 1), ("gy", 2)), REACH)
    weights_grown = with_halo(pair_weight, (("gx", 1), ("gy", 2)), REACH)
    tables_grown = build_tables(codes_grown, weights_grown)
    multiplier = jnp.zeros((face_rows, face_cols), jnp.float32)
    multiplier_grown = jnp.zeros((grown_rows, grown_cols), jnp.float32)
    solution = jnp.zeros_like(load)
    interface_load = jnp.zeros_like(load)
    for outer_step in range(UZAWA):
        residual = load + interface_load - operate(solution)
        image = operate(residual)
        norm_now, product = two_products(residual, image)
        alpha = norm_now / product
        direction, along = (residual, image)
        for inner_step in range(INNER):
            solution = solution + alpha * direction
            residual = residual - alpha * along
            if inner_step + 1 < INNER:
                image = operate(residual)
                norm_next, product = two_products(residual, image)
                ratio = norm_next / norm_now
                alpha = norm_next / (product - ratio * norm_next / alpha)
                direction = residual + ratio * direction
                along = image + ratio * along
                norm_now = norm_next
        master_top = solution[layers - 1]
        slave_bottom = passed_along(solution[0], "body", -1)
        face_pair = with_halo(
            jnp.stack([master_top, slave_bottom]), (("gx", 1), ("gy", 2)), 2 * REACH
        )
        pulled = pull_sum(tables_grown, face_pair[0], grown_rows, grown_cols)
        slave_grown = face_pair[1, REACH : REACH + grown_rows, REACH : REACH + grown_cols]
        multiplier_grown = jnp.where(
            has_above, multiplier_grown + RATE * (slave_grown - pulled), 0.0
        )
        multiplier = multiplier_grown[REACH : REACH + face_rows, REACH : REACH + face_cols]
        force = push_sum(tables_grown, multiplier_grown, face_rows, face_cols)
        lifted = passed_along(multiplier, "body", 1)
        interface_load = jnp.where(top_layer, force[None], 0.0) + jnp.where(
            bottom_layer, -lifted[None], 0.0
        )
    return (solution, interface_load)


def solution(mesh):
    return jax.shard_map(
        per_device,
        mesh=mesh,
        in_specs=(
            P("body", "gx", "gy"),
            P("body", "gx", "gy"),
            P(None, "gx", "gy"),
            P(None, "gx", "gy"),
        ),
        out_specs=(P("body", "gx", "gy"), P("body", "gx", "gy")),
        check_vma=False,
    )
```

profile of v0, /device:TPU:1, one launch (start us, length us, event | category | flops | bytes accessed | tf_op | source)
XLA Modules:
  0.0 341.6 jit_solution(11003842452371431871)
XLA Ops:
  0.6 5.1 %collective-permute-start.1 = (f32[16,1,128]{2,0,1:T(8,128)S(1)}, f32[16,1,128]{2,0,1:T(8,128)S(1)}, u32[]{:S(2)}, u32[]{:S(2)}) collective-permute-start(f32[16,1,128]{2,0,1:T(8,128)S(1)} %broadcast.56), channel_id=1, source_target_pairs={{4,0},{8,4},{12,8},{16,12},{20,16},{24,20},{28,24},{5,1},{9,5},{13... | collective-permute-start | bytes 24584 | tf_op jit(solution)/shard_map/ppermute | solution.py:24
  11.0 4.0 %collective-permute-start.2 = (f32[16,66,1]{1,0,2:T(8,128)S(1)}, f32[16,66,1]{1,0,2:T(8,128)S(1)}, u32[]{:S(2)}, u32[]{:S(2)}) collective-permute-start(f32[16,66,1]{1,0,2:T(8,128)S(1)} %copy.204), channel_id=1, source_target_pairs={{0,1},{1,2},{2,3},{4,5},{5,6},{6,7},{8,9},{9,10},{10,11},{12,13},{... | collective-permute-start | bytes 12680 | tf_op jit(solution)/shard_map/ppermute | solution.py:22
  21.3 3.7 %collective-permute-start.4 = (f32[16,1,128]{2,0,1:T(8,128)S(1)}, f32[16,1,128]{2,0,1:T(8,128)S(1)}, u32[]{:S(2)}, u32[]{:S(2)}) collective-permute-start(f32[16,1,128]{2,0,1:T(8,128)S(1)} %bitcast.131), channel_id=1, source_target_pairs={{0,4},{4,8},{8,12},{12,16},{16,20},{20,24},{24,28},{1,5},{5,9},{9,... | collective-permute-start | bytes 24584 | tf_op jit(solution)/shard_map/ppermute | solution.py:22
  26.6 3.9 %collective-permute-start.6 = (f32[16,66,1]{1,0,2:T(8,128)S(1)}, f32[16,66,1]{1,0,2:T(8,128)S(1)}, u32[]{:S(2)}, u32[]{:S(2)}) collective-permute-start(f32[16,66,1]{1,0,2:T(8,128)S(1)} %copy.216), channel_id=1, source_target_pairs={{0,1},{1,2},{2,3},{4,5},{5,6},{6,7},{8,9},{9,10},{10,11},{12,13},{... | collective-permute-start | bytes 12680 | tf_op jit(solution)/shard_map/ppermute | solution.py:22
  31.8 4.5 %collective-permute-start.20 = (f32[4,2,128]{2,1,0:T(2,128)S(1)}, f32[4,2,128]{2,1,0:T(2,128)S(1)}, u32[]{:S(2)}, u32[]{:S(2)}) collective-permute-start(f32[4,2,128]{2,1,0:T(2,128)S(1)} %get-tuple-element.85), channel_id=1, source_target_pairs={{0,4},{4,8},{8,12},{12,16},{16,20},{20,24},{24,28},{1,5},{5,9},{9,... | collective-permute-start | bytes 12296 | tf_op jit(solution)/shard_map/ppermute | solution.py:22
  42.9 8.3 %all-to-all-start = ((f32[32,1,2]{2,1,0:T(1,128)}), f32[32,1,2]{2,1,0:T(1,128)S(1)}, u32[]{:S(2)}, u32[]{:S(2)}) async-start(f32[32,1,2]{2,1,0:T(1,128)} %broadcast_in_dim.87), calls=%async_computation | async-start | bytes 32768 | tf_op jit(solution)/shard_map/all_to_all | solution.py:33
  84.5 7.0 %all-to-all-start.1 = ((f32[32,1,2]{2,1,0:T(1,128)}), f32[32,1,2]{2,1,0:T(1,128)S(1)}, u32[]{:S(2)}, u32[]{:S(2)}) async-start(f32[32,1,2]{2,1,0:T(1,128)} %broadcast_in_dim.88), calls=%async_computation.1 | async-start | bytes 32768 | tf_op jit(solution)/shard_map/all_to_all | solution.py:33
  92.2 6.2 %all-to-all-done.1 = f32[32,1,2]{2,1,0:T(1,128)S(1)} async-done(((f32[32,1,2]{2,1,0:T(1,128)}), f32[32,1,2]{2,1,0:T(1,128)S(1)}, u32[]{:S(2)}, u32[]{:S(2)}) %all-to-all-start.1) | async-done | bytes 288 | tf_op jit(solution)/shard_map/all_to_all | solution.py:33
  126.9 7.7 %all-to-all-start.2 = ((f32[32,1,2]{2,1,0:T(1,128)}), f32[32,1,2]{2,1,0:T(1,128)S(1)}, u32[]{:S(2)}, u32[]{:S(2)}) async-start(f32[32,1,2]{2,1,0:T(1,128)} %broadcast_in_dim.89), calls=%async_computation.2 | async-start | bytes 32768 | tf_op jit(solution)/shard_map/all_to_all | solution.py:33
  139.1 4.0 %collective-permute-start.22 = (f32[4,68,2]{2,1,0:T(8,128)S(1)}, f32[4,68,2]{2,1,0:T(8,128)S(1)}, u32[]{:S(2)}, u32[]{:S(2)}) collective-permute-start(f32[4,68,2]{2,1,0:T(8,128)S(1)} %copy-done.60), channel_id=1, source_target_pairs={{0,1},{1,2},{2,3},{4,5},{5,6},{6,7},{8,9},{9,10},{10,11},{12,13},{... | collective-permute-start | bytes 6536 | tf_op jit(solution)/shard_map/ppermute | solution.py:22
  160.6 4.1 %collective-permute-start.32 = (f32[16,66,1]{1,0,2:T(8,128)S(1)}, f32[16,66,1]{1,0,2:T(8,128)S(1)}, u32[]{:S(2)}, u32[]{:S(2)}) collective-permute-start(f32[16,66,1]{1,0,2:T(8,128)S(1)} %copy.255), channel_id=1, source_target_pairs={{0,1},{1,2},{2,3},{4,5},{5,6},{6,7},{8,9},{9,10},{10,11},{12,13},{... | collective-permute-start | bytes 12680 | tf_op jit(solution)/shard_map/ppermute | solution.py:22
  166.1 3.7 %collective-permute-start.25 = (f32[2,4,128]{2,1,0:T(4,128)S(1)}, f32[2,4,128]{2,1,0:T(4,128)S(1)}, u32[]{:S(2)}, u32[]{:S(2)}) collective-permute-start(f32[2,4,128]{2,1,0:T(4,128)S(1)} %get-tuple-element.93), channel_id=1, source_target_pairs={{0,4},{4,8},{8,12},{12,16},{16,20},{20,24},{24,28},{1,5},{5,9},{9,... | collective-permute-start | bytes 12296 | tf_op jit(solution)/shard_map/ppermute | solution.py:22
  176.8 4.3 %collective-permute-start.27 = (f32[2,72,4]{2,1,0:T(8,128)S(1)}, f32[2,72,4]{2,1,0:T(8,128)S(1)}, u32[]{:S(2)}, u32[]{:S(2)}) collective-permute-start(f32[2,72,4]{2,1,0:T(8,128)S(1)} %get-tuple-element.89), channel_id=1, source_target_pairs={{0,1},{1,2},{2,3},{4,5},{5,6},{6,7},{8,9},{9,10},{10,11},{12,13},{... | collective-permute-start | bytes 6920 | tf_op jit(solution)/shard_map/ppermute | solution.py:22
  187.2 3.7 %collective-permute-start.29 = (f32[64,128]{1,0:T(8,128)S(1)}, f32[64,128]{1,0:T(8,128)S(1)}, u32[]{:S(2)}, u32[]{:S(2)}) collective-permute-start(f32[64,128]{1,0:T(8,128)S(1)} %slice.978), channel_id=1, source_target_pairs={{0,32},{32,64},{64,96},{96,128},{128,160},{160,192},{192,224},{1,3... | collective-permute-start | bytes 98312 | tf_op jit(solution)/shard_map/ppermute | solution.py:52
  194.8 5.8 %collective-permute-start.34 = (f32[16,1,128]{2,0,1:T(8,128)S(1)}, f32[16,1,128]{2,0,1:T(8,128)S(1)}, u32[]{:S(2)}, u32[]{:S(2)}) collective-permute-start(f32[16,1,128]{2,0,1:T(8,128)S(1)} %bitcast.133), channel_id=1, source_target_pairs={{0,4},{4,8},{8,12},{12,16},{16,20},{20,24},{24,28},{1,5},{5,9},{9,... | collective-permute-start | bytes 24584 | tf_op jit(solution)/shard_map/ppermute | solution.py:22
  203.5 4.0 %collective-permute-start.36 = (f32[16,66,1]{1,0,2:T(8,128)S(1)}, f32[16,66,1]{1,0,2:T(8,128)S(1)}, u32[]{:S(2)}, u32[]{:S(2)}) collective-permute-start(f32[16,66,1]{1,0,2:T(8,128)S(1)} %copy.267), channel_id=1, source_target_pairs={{0,1},{1,2},{2,3},{4,5},{5,6},{6,7},{8,9},{9,10},{10,11},{12,13},{... | collective-permute-start | bytes 12680 | tf_op jit(solution)/shard_map/ppermute | solution.py:22
  212.1 16.8 %all_to_all.36 = f32[32,1,2]{2,1,0:T(1,128)S(1)} all-to-all(f32[32,1,2]{2,1,0:T(1,128)S(1)} %broadcast_in_dim.94), channel_id=1, replica_groups=mesh['body'=8,'gx'=8,'gy'=4] {'gx','gy'}, dimensions={0} | all-to-all | bytes 512 | tf_op jit(solution)/shard_map/all_to_all | solution.py:33
  241.1 4.0 %collective-permute-start.40 = (f32[16,66,1]{1,0,2:T(8,128)S(1)}, f32[16,66,1]{1,0,2:T(8,128)S(1)}, u32[]{:S(2)}, u32[]{:S(2)}) collective-permute-start(f32[16,66,1]{1,0,2:T(8,128)S(1)} %copy.280), channel_id=1, source_target_pairs={{0,1},{1,2},{2,3},{4,5},{5,6},{6,7},{8,9},{9,10},{10,11},{12,13},{... | collective-permute-start | bytes 12680 | tf_op jit(solution)/shard_map/ppermute | solution.py:22
  250.4 15.0 %all_to_all.37 = f32[32,1,2]{2,1,0:T(1,128)S(1)} all-to-all(f32[32,1,2]{2,1,0:T(1,128)S(1)} %broadcast_in_dim.95), channel_id=1, replica_groups=mesh['body'=8,'gx'=8,'gy'=4] {'gx','gy'}, dimensions={0} | all-to-all | bytes 512 | tf_op jit(solution)/shard_map/all_to_all | solution.py:33
  282.3 4.0 %collective-permute-start.44 = (f32[16,66,1]{1,0,2:T(8,128)S(1)}, f32[16,66,1]{1,0,2:T(8,128)S(1)}, u32[]{:S(2)}, u32[]{:S(2)}) collective-permute-start(f32[16,66,1]{1,0,2:T(8,128)S(1)} %copy.293), channel_id=1, source_target_pairs={{0,1},{1,2},{2,3},{4,5},{5,6},{6,7},{8,9},{9,10},{10,11},{12,13},{... | collective-permute-start | bytes 12680 | tf_op jit(solution)/shard_map/ppermute | solution.py:22
  292.7 15.0 %all_to_all.38 = f32[32,1,2]{2,1,0:T(1,128)S(1)} all-to-all(f32[32,1,2]{2,1,0:T(1,128)S(1)} %broadcast_in_dim.96), channel_id=1, replica_groups=mesh['body'=8,'gx'=8,'gy'=4] {'gx','gy'}, dimensions={0} | all-to-all | bytes 512 | tf_op jit(solution)/shard_map/all_to_all | solution.py:33
  314.3 3.9 %collective-permute-done.46 = f32[64,128]{1,0:T(8,128)S(1)} collective-permute-done((f32[64,128]{1,0:T(8,128)S(1)}, f32[64,128]{1,0:T(8,128)S(1)}, u32[]{:S(2)}, u32[]{:S(2)}) %collective-permute-start.46) | collective-permute-done | bytes 32800 | tf_op jit(solution)/shard_map/ppermute | solution.py:52
  330.5 3.7 %collective-permute-done.50 = f32[2,72,4]{2,1,0:T(8,128)S(1)} collective-permute-done((f32[2,72,4]{2,1,0:T(8,128)S(1)}, f32[2,72,4]{2,1,0:T(8,128)S(1)}, u32[]{:S(2)}, u32[]{:S(2)}) %collective-permute-start.50) | collective-permute-done | bytes 2336 | tf_op jit(solution)/shard_map/ppermute | solution.py:24
  335.2 4.3 %collective-permute-start.51 = (f32[64,128]{1,0:T(8,128)S(1)}, f32[64,128]{1,0:T(8,128)S(1)}, u32[]{:S(2)}, u32[]{:S(2)}) collective-permute-start(f32[64,128]{1,0:T(8,128)S(1)} %slice.1084), channel_id=1, source_target_pairs={{0,32},{32,64},{64,96},{96,128},{128,160},{160,192},{192,224},{1,3... | collective-permute-start | bytes 98312 | tf_op jit(solution)/shard_map/ppermute | solution.py:52
  (365 shorter events, 173.0 us)
Async XLA Ops:
  0.6 7.0 %collective-permute-start.1 = (f32[16,1,128]{2,0,1:T(8,128)S(1)}, f32[16,1,128]{2,0,1:T(8,128)S(1)}, u32[]{:S(2)}, u32[]{:S(2)}) collective-permute-start(f32[16,1,128]{2,0,1:T(8,128)S(1)} %broadcast.56), channel_id=1, source_target_pairs={{4,0},{8,4},{12,8},{16,12},{20,16},{24,20},{28,24},{5,1},{9,5},{13... | collective-permute-start | bytes 24584 | tf_op jit(solution)/shard_map/ppermute | solution.py:24
  18.1 6.9 %collective-permute-start.5 = (f32[16,1,128]{2,0,1:T(8,128)S(1)}, f32[16,1,128]{2,0,1:T(8,128)S(1)}, u32[]{:S(2)}, u32[]{:S(2)}) collective-permute-start(f32[16,1,128]{2,0,1:T(8,128)S(1)} %bitcast.136), channel_id=1, source_target_pairs={{4,0},{8,4},{12,8},{16,12},{20,16},{24,20},{28,24},{5,1},{9,5},{13... | collective-permute-start | bytes 24584 | tf_op jit(solution)/shard_map/ppermute | solution.py:24
  26.6 12.0 %collective-permute-start.6 = (f32[16,66,1]{1,0,2:T(8,128)S(1)}, f32[16,66,1]{1,0,2:T(8,128)S(1)}, u32[]{:S(2)}, u32[]{:S(2)}) collective-permute-start(f32[16,66,1]{1,0,2:T(8,128)S(1)} %copy.216), channel_id=1, source_target_pairs={{0,1},{1,2},{2,3},{4,5},{5,6},{6,7},{8,9},{9,10},{10,11},{12,13},{... | collective-permute-start | bytes 12680 | tf_op jit(solution)/shard_map/ppermute | solution.py:22
  30.5 7.7 %collective-permute-start.7 = (f32[16,66,1]{1,0,2:T(8,128)S(1)}, f32[16,66,1]{1,0,2:T(8,128)S(1)}, u32[]{:S(2)}, u32[]{:S(2)}) collective-permute-start(f32[16,66,1]{1,0,2:T(8,128)S(1)} %copy.217), channel_id=1, source_target_pairs={{1,0},{2,1},{3,2},{5,4},{6,5},{7,6},{9,8},{10,9},{11,10},{13,12},{... | collective-permute-start | bytes 12680 | tf_op jit(solution)/shard_map/ppermute | solution.py:24
  31.8 41.1 %collective-permute-start.20 = (f32[4,2,128]{2,1,0:T(2,128)S(1)}, f32[4,2,128]{2,1,0:T(2,128)S(1)}, u32[]{:S(2)}, u32[]{:S(2)}) collective-permute-start(f32[4,2,128]{2,1,0:T(2,128)S(1)} %get-tuple-element.85), channel_id=1, source_target_pairs={{0,4},{4,8},{8,12},{12,16},{16,20},{20,24},{24,28},{1,5},{5,9},{9,... | collective-permute-start | bytes 12296 | tf_op jit(solution)/shard_map/ppermute | solution.py:22
  36.3 37.9 %collective-permute-start.21 = (f32[4,2,128]{2,1,0:T(2,128)S(1)}, f32[4,2,128]{2,1,0:T(2,128)}, u32[]{:S(2)}, u32[]{:S(2)}) collective-permute-start(f32[4,2,128]{2,1,0:T(2,128)S(1)} %get-tuple-element.86), channel_id=1, source_target_pairs={{4,0},{8,4},{12,8},{16,12},{20,16},{24,20},{28,24},{5,1},{9,5},{13... | collective-permute-start | bytes 12296 | tf_op jit(solution)/shard_map/ppermute | solution.py:24
  42.9 15.2 %all-to-all-start = ((f32[32,1,2]{2,1,0:T(1,128)}), f32[32,1,2]{2,1,0:T(1,128)S(1)}, u32[]{:S(2)}, u32[]{:S(2)}) async-start(f32[32,1,2]{2,1,0:T(1,128)} %broadcast_in_dim.87), calls=%async_computation | async-start | bytes 32768 | tf_op jit(solution)/shard_map/all_to_all | solution.py:33
  52.5 57.7 %collective-permute-start.16 = (s32[4,2,128]{2,1,0:T(2,128)}, s32[4,2,128]{2,1,0:T(2,128)}, u32[]{:S(2)}, u32[]{:S(2)}) collective-permute-start(s32[4,2,128]{2,1,0:T(2,128)} %get-tuple-element.83), channel_id=1, source_target_pairs={{0,4},{4,8},{8,12},{12,16},{16,20},{20,24},{24,28},{1,5},{5,9},{9,... | collective-permute-start | bytes 12296 | tf_op jit(solution)/shard_map/ppermute | solution.py:22
  66.3 44.0 %collective-permute-start.17 = (s32[4,2,128]{2,1,0:T(2,128)}, s32[4,2,128]{2,1,0:T(2,128)}, u32[]{:S(2)}, u32[]{:S(2)}) collective-permute-start(s32[4,2,128]{2,1,0:T(2,128)} %get-tuple-element.84), channel_id=1, source_target_pairs={{4,0},{8,4},{12,8},{16,12},{20,16},{24,20},{28,24},{5,1},{9,5},{13... | collective-permute-start | bytes 12296 | tf_op jit(solution)/shard_map/ppermute | solution.py:24
  70.2 7.7 %collective-permute-start.10 = (f32[16,66,1]{1,0,2:T(8,128)S(1)}, f32[16,66,1]{1,0,2:T(8,128)}, u32[]{:S(2)}, u32[]{:S(2)}) collective-permute-start(f32[16,66,1]{1,0,2:T(8,128)S(1)} %copy.229), channel_id=1, source_target_pairs={{0,1},{1,2},{2,3},{4,5},{5,6},{6,7},{8,9},{9,10},{10,11},{12,13},{... | collective-permute-start | bytes 12680 | tf_op jit(solution)/shard_map/ppermute | solution.py:22
  84.5 13.9 %all-to-all-start.1 = ((f32[32,1,2]{2,1,0:T(1,128)}), f32[32,1,2]{2,1,0:T(1,128)S(1)}, u32[]{:S(2)}, u32[]{:S(2)}) async-start(f32[32,1,2]{2,1,0:T(1,128)} %broadcast_in_dim.88), calls=%async_computation.1 | async-start | bytes 32768 | tf_op jit(solution)/shard_map/all_to_all | solution.py:33
  104.6 6.3 %collective-permute-start.13 = (f32[16,1,128]{2,0,1:T(8,128)S(1)}, f32[16,1,128]{2,0,1:T(8,128)S(1)}, u32[]{:S(2)}, u32[]{:S(2)}) collective-permute-start(f32[16,1,128]{2,0,1:T(8,128)S(1)} %bitcast.130), channel_id=1, source_target_pairs={{4,0},{8,4},{12,8},{16,12},{20,16},{24,20},{28,24},{5,1},{9,5},{13... | collective-permute-start | bytes 24584 | tf_op jit(solution)/shard_map/ppermute | solution.py:24
  113.6 6.9 %collective-permute-start.14 = (f32[16,66,1]{1,0,2:T(8,128)S(1)}, f32[16,66,1]{1,0,2:T(8,128)S(1)}, u32[]{:S(2)}, u32[]{:S(2)}) collective-permute-start(f32[16,66,1]{1,0,2:T(8,128)S(1)} %copy.242), channel_id=1, source_target_pairs={{0,1},{1,2},{2,3},{4,5},{5,6},{6,7},{8,9},{9,10},{10,11},{12,13},{... | collective-permute-start | bytes 12680 | tf_op jit(solution)/shard_map/ppermute | solution.py:22
  126.9 16.3 %all-to-all-start.2 = ((f32[32,1,2]{2,1,0:T(1,128)}), f32[32,1,2]{2,1,0:T(1,128)S(1)}, u32[]{:S(2)}, u32[]{:S(2)}) async-start(f32[32,1,2]{2,1,0:T(1,128)} %broadcast_in_dim.89), calls=%async_computation.2 | async-start | bytes 32768 | tf_op jit(solution)/shard_map/all_to_all | solution.py:33
  134.6 30.2 %collective-permute-start.18 = (s32[4,68,2]{2,1,0:T(8,128)}, s32[4,68,2]{2,1,0:T(8,128)S(1)}, u32[]{:S(2)}, u32[]{:S(2)}) collective-permute-start(s32[4,68,2]{2,1,0:T(8,128)} %get-tuple-element.79), channel_id=1, source_target_pairs={{0,1},{1,2},{2,3},{4,5},{5,6},{6,7},{8,9},{9,10},{10,11},{12,13},{... | collective-permute-start | bytes 6536 | tf_op jit(solution)/shard_map/ppermute | solution.py:22
  137.8 28.3 %collective-permute-start.19 = (s32[4,68,2]{2,1,0:T(8,128)}, s32[4,68,2]{2,1,0:T(8,128)S(1)}, u32[]{:S(2)}, u32[]{:S(2)}) collective-permute-start(s32[4,68,2]{2,1,0:T(8,128)} %get-tuple-element.80), channel_id=1, source_target_pairs={{1,0},{2,1},{3,2},{5,4},{6,5},{7,6},{9,8},{10,9},{11,10},{13,12},{... | collective-permute-start | bytes 6536 | tf_op jit(solution)/shard_map/ppermute | solution.py:24
  139.1 30.7 %collective-permute-start.22 = (f32[4,68,2]{2,1,0:T(8,128)S(1)}, f32[4,68,2]{2,1,0:T(8,128)S(1)}, u32[]{:S(2)}, u32[]{:S(2)}) collective-permute-start(f32[4,68,2]{2,1,0:T(8,128)S(1)} %copy-done.60), channel_id=1, source_target_pairs={{0,1},{1,2},{2,3},{4,5},{5,6},{6,7},{8,9},{9,10},{10,11},{12,13},{... | collective-permute-start | bytes 6536 | tf_op jit(solution)/shard_map/ppermute | solution.py:22
  154.0 17.8 %collective-permute-start.23 = (f32[4,68,2]{2,1,0:T(8,128)S(1)}, f32[4,68,2]{2,1,0:T(8,128)}, u32[]{:S(2)}, u32[]{:S(2)}) collective-permute-start(f32[4,68,2]{2,1,0:T(8,128)S(1)} %copy-done.59), channel_id=1, source_target_pairs={{1,0},{2,1},{3,2},{5,4},{6,5},{7,6},{9,8},{10,9},{11,10},{13,12},{... | collective-permute-start | bytes 6536 | tf_op jit(solution)/shard_map/ppermute | solution.py:24
  160.6 14.9 %collective-permute-start.32 = (f32[16,66,1]{1,0,2:T(8,128)S(1)}, f32[16,66,1]{1,0,2:T(8,128)S(1)}, u32[]{:S(2)}, u32[]{:S(2)}) collective-permute-start(f32[16,66,1]{1,0,2:T(8,128)S(1)} %copy.255), channel_id=1, source_target_pairs={{0,1},{1,2},{2,3},{4,5},{5,6},{6,7},{8,9},{9,10},{10,11},{12,13},{... | collective-permute-start | bytes 12680 | tf_op jit(solution)/shard_map/ppermute | solution.py:22
  164.8 10.4 %collective-permute-start.33 = (f32[16,66,1]{1,0,2:T(8,128)S(1)}, f32[16,66,1]{1,0,2:T(8,128)S(1)}, u32[]{:S(2)}, u32[]{:S(2)}) collective-permute-start(f32[16,66,1]{1,0,2:T(8,128)S(1)} %copy.256), channel_id=1, source_target_pairs={{1,0},{2,1},{3,2},{5,4},{6,5},{7,6},{9,8},{10,9},{11,10},{13,12},{... | collective-permute-start | bytes 12680 | tf_op jit(solution)/shard_map/ppermute | solution.py:24
  166.1 9.8 %collective-permute-start.25 = (f32[2,4,128]{2,1,0:T(4,128)S(1)}, f32[2,4,128]{2,1,0:T(4,128)S(1)}, u32[]{:S(2)}, u32[]{:S(2)}) collective-permute-start(f32[2,4,128]{2,1,0:T(4,128)S(1)} %get-tuple-element.93), channel_id=1, source_target_pairs={{0,4},{4,8},{8,12},{12,16},{16,20},{20,24},{24,28},{1,5},{5,9},{9,... | collective-permute-start | bytes 12296 | tf_op jit(solution)/shard_map/ppermute | solution.py:22
  176.8 6.4 %collective-permute-start.27 = (f32[2,72,4]{2,1,0:T(8,128)S(1)}, f32[2,72,4]{2,1,0:T(8,128)S(1)}, u32[]{:S(2)}, u32[]{:S(2)}) collective-permute-start(f32[2,72,4]{2,1,0:T(8,128)S(1)} %get-tuple-element.89), channel_id=1, source_target_pairs={{0,1},{1,2},{2,3},{4,5},{5,6},{6,7},{8,9},{9,10},{10,11},{12,13},{... | collective-permute-start | bytes 6920 | tf_op jit(solution)/shard_map/ppermute | solution.py:22
  192.8 7.9 %collective-permute-start.35 = (f32[16,1,128]{2,0,1:T(8,128)S(1)}, f32[16,1,128]{2,0,1:T(8,128)S(1)}, u32[]{:S(2)}, u32[]{:S(2)}) collective-permute-start(f32[16,1,128]{2,0,1:T(8,128)S(1)} %bitcast.137), channel_id=1, source_target_pairs={{4,0},{8,4},{12,8},{16,12},{20,16},{24,20},{28,24},{5,1},{9,5},{13... | collective-permute-start | bytes 24584 | tf_op jit(solution)/shard_map/ppermute | solution.py:24
  194.8 6.6 %collective-permute-start.34 = (f32[16,1,128]{2,0,1:T(8,128)S(1)}, f32[16,1,128]{2,0,1:T(8,128)S(1)}, u32[]{:S(2)}, u32[]{:S(2)}) collective-permute-start(f32[16,1,128]{2,0,1:T(8,128)S(1)} %bitcast.133), channel_id=1, source_target_pairs={{0,4},{4,8},{8,12},{12,16},{16,20},{20,24},{24,28},{1,5},{5,9},{9,... | collective-permute-start | bytes 24584 | tf_op jit(solution)/shard_map/ppermute | solution.py:22
  (103 other events, 1144.0 us)
where the time goes:
time: 346 us; the launch traced here: 342 us
  starting transfers between devices  165 us (48%)
  blocking collectives  46.8 us (14%)
  other arithmetic  40.8 us (12%)
  waiting for transfers between devices  37.4 us (11%)
  local copies, waits for them, and re-layouts  29.4 us (8%)
  between operations  22.1 us (6%)
    ppermute x24, starting transfers between devices, with_halo(): lax.ppermute(tail, axis, [(i, (i + 1) % count) for i in range(ends)])  84.5 us
    ppermute x24, starting transfers between devices, with_halo(): lax.ppermute(head, axis, [((i + 1) % count, i) for i in range(ends)])  47 us
    all_to_all x3, blocking collectives, sent_to_all(): return lax.all_to_all(copies, axis, split_axis=0, concat_axis=0, tiled=True)  46.8 us
    all_to_all x3, starting transfers between devices, sent_to_all(): return lax.all_to_all(copies, axis, split_axis=0, concat_axis=0, tiled=True)  22.9 us
    ppermute x24, waiting for transfers between devices, with_halo(): lax.ppermute(head, axis, [((i + 1) % count, i) for i in range(ends)])  14.8 us
    concatenate x22, other arithmetic, with_halo(): jnp.concatenate([lax.ppermute(tail, axis, [(i, (i + 1) % count) for i in...  10.8 us
    ppermute x4, starting transfers between devices, passed_along(): return lax.ppermute(array, axis, pairs)  10.7 us
    reduce_sum x6, other arithmetic, two_products(): jnp.sum(residual * residual)  10.3 us
  transfers between devices with their start and end apart: 55, of which 21 were waited for; matrix products, arithmetic and copies ran while one was open for 9% of the time, Pallas kernels for 0%

commit v1 on v0

v1 whole, which is shorter than its diff:
```python
import functools

import jax
import jax.numpy as jnp
from jax import lax
from jax.experimental import pallas as pl
from jax.experimental.pallas import tpu as pltpu
from jax.sharding import PartitionSpec as P

MESH = pl.DeviceIdType.MESH
F32 = jnp.float32

NBODY, NGX, NGY = 8, 8, 4
NPEER = NGX * NGY
CZ, BR, BC = 16, 64, 128
REACH, SPAN, RATE = 2, 5, 2.0
OFF = 24
ROWS = BR + 2 * OFF
LO, HI = 8, ROWS - 8
NLO, NHI = 16, ROWS - 16
W = 12
SLOTS = 10
SHIFT = 6.0


def roll(x, by):
    by %= BC
    return x if by == 0 else pltpu.roll(x, by, x.ndim - 1)


def lanes(shape):
    return lax.broadcasted_iota(jnp.int32, shape, len(shape) - 1)


def moved(a, b, by):
    if by == 0:
        return a, b
    lane = lanes(a.shape)
    late = lane < by if by > 0 else lane >= BC + by
    return roll(jnp.where(late, b, a), -by), roll(jnp.where(late, a, b), -by)


def chunks(first, last, step):
    return [(r, min(step, last - r)) for r in range(first, last, step)]


def kernel(
    load, stiff, code, weight, sol, ifl,
    va, vb, ua, ub, sa, sb, ci, ca, cb, wa, wb, sl, sr, pl_, pr, ta, tb,
    sha, shb, fa, fb, ma, mb, stage, fdn, fup, gdn, gup, mrow, mbuf, mz,
    lsem, rs, rr, fs, fr, gs, gr, as_, ar, zs, zr,
):
    body, gx, gy = (lax.axis_index(n) for n in ("body", "gx", "gy"))
    me = gx * NGY + gy
    gxm, gxp = lax.rem(gx + NGX - 1, NGX), lax.rem(gx + 1, NGX)
    gym, gyp = lax.rem(gy + NGY - 1, NGY), lax.rem(gy + 1, NGY)
    below, above = lax.rem(body + NBODY - 1, NBODY), lax.rem(body + 1, NBODY)

    def peer(o):
        p = lax.rem(me + o, NPEER)
        return (body, p // NGY, lax.rem(p, NGY))

    barrier = pltpu.get_barrier_semaphore()

    def greet(o, carry):
        pl.semaphore_signal(barrier, inc=1, device_id=peer(o), device_id_type=MESH)
        return carry

    locals_ = [
        pltpu.make_async_copy(load, va.at[0, pl.ds(1, CZ), pl.ds(OFF, BR), :], lsem.at[0]),
        pltpu.make_async_copy(stiff, sa.at[:, pl.ds(OFF, BR), :], lsem.at[1]),
        pltpu.make_async_copy(code, ci.at[:, pl.ds(OFF, BR), :], lsem.at[2]),
        pltpu.make_async_copy(weight, wa.at[:, pl.ds(OFF, BR), :], lsem.at[3]),
    ]
    for c in locals_:
        c.start()
    lax.fori_loop(1, NPEER, greet, 0)
    pl.semaphore_signal(barrier, inc=1, device_id=(below, gx, gy), device_id_type=MESH)
    pl.semaphore_signal(barrier, inc=1, device_id=(above, gx, gy), device_id_type=MESH)

    one = jnp.float32(1.0)
    zero = jnp.float32(0.0)
    top_ok = jnp.where(gx > 0, one, zero)
    bot_ok = jnp.where(gx < NGX - 1, one, zero)
    right_ok = jnp.where(gy < NGY - 1, one, zero)
    left_ok = jnp.where(gy > 0, one, zero)
    up_ok = jnp.where(body < NBODY - 1, one, zero)
    dn_ok = jnp.where(body > 0, one, zero)

    zl = jnp.zeros((ROWS, BC), F32)
    for k in range(4):
        for l in (0, CZ + 1):
            va[k, l] = zl
            vb[k, l] = zl
            if k < 3:
                ua[k, l] = zl
                ub[k, l] = zl
    z8 = jnp.zeros((8, BC), F32)
    for l in range(2, 13):
        for r in (LO, NHI):
            va[0, 1 + l, r : r + 8] = z8
            sa[l, r : r + 8] = z8
    for k in range(4):
        for r in (LO, NHI):
            wa[k, r : r + 8] = z8

    for c in locals_:
        c.wait()

    def item(q, r):
        if q < CZ:
            return va[0, 1 + q, pl.ds(r, 8), :]
        if q < 2 * CZ:
            return sa[q - CZ, pl.ds(r, 8), :]
        if q < 2 * CZ + 4:
            return ci[q - 2 * CZ, pl.ds(r, 8), :].astype(F32)
        return wa[q - 2 * CZ - 4, pl.ds(r, 8), :]

    lane8 = lanes((8, BC))

    def pack(t, carry):
        o = pl.multiple_of(8 * t, 8)
        r = pl.multiple_of(8 * t + OFF, 8)
        for j in range(4):
            left = right = None
            for s in range(SLOTS):
                x = item(SLOTS * j + s, r)
                xl, xr = roll(x, W * s), roll(x, W * s + W)
                left = xl if s == 0 else jnp.where(lane8 >= W * s, xl, left)
                right = xr if s == 0 else jnp.where(lane8 >= W * s, xr, right)
            sl[j, pl.ds(o, 8), :] = left
            sr[j, pl.ds(o, 8), :] = right
        return carry

    lax.fori_loop(0, BR // 8, pack, 0)

    pl.semaphore_wait(barrier, NPEER - 1 + 2)

    sends = []

    def send(src, dst, dev):
        n = len(sends)
        c = pltpu.make_async_remote_copy(src, dst, rs.at[n], rr.at[n], device_id=dev, device_id_type=MESH)
        c.start()
        sends.append(c)

    def column_sends(buf, dst, dev_y):
        send(buf.at[:, pl.ds(0, BR), :], dst.at[:, pl.ds(OFF, BR), :], (body, gx, dev_y))

    def corner_sends(buf, dst, dev_y):
        send(buf.at[:, pl.ds(0, 16), :], dst.at[:, pl.ds(OFF + BR, 16), :], (body, gxm, dev_y))
        send(buf.at[:, pl.ds(BR - 16, 16), :], dst.at[:, pl.ds(LO, 16), :], (body, gxp, dev_y))

    column_sends(sl, pr, gym)
    column_sends(sr, pl_, gyp)
    for dev, near, to_near, far, to_far in (
        ((body, gxm, gy), OFF, OFF + BR, OFF + 8, OFF + BR + 8),
        ((body, gxp, gy), OFF + BR - 8, NLO, OFF + BR - 16, LO),
    ):
        for ref, lead in ((va, (0,)), (sa, ())):
            base = 1 if lead else 0

            def part(l, n, r):
                return ref.at[lead + (pl.ds(base + l, n), pl.ds(r, 8), slice(None))]

            send(part(0, CZ, near), part(0, CZ, to_near), dev)
            send(part(0, 2, far), part(0, 2, to_far), dev)
            send(part(13, 3, far), part(13, 3, to_far), dev)
        send(ci.at[:, pl.ds(near, 8), :], ci.at[:, pl.ds(to_near, 8), :], dev)
        send(wa.at[:, pl.ds(near, 8), :], wa.at[:, pl.ds(to_near, 8), :], dev)
    corner_sends(sl, pr, gym)
    corner_sends(sr, pl_, gyp)
    for c in sends:
        c.wait_recv()

    right_lane = lane8 < W
    left_lane = lane8 >= BC - W
    lane_ok = jnp.where(lane8 < BC // 2, right_ok, left_ok)

    def unpack(t, carry):
        r = pl.multiple_of(8 * t + LO, 8)
        row_ok = jnp.where(t < 2, top_ok, jnp.where(t >= 10, bot_ok, one))
        ok = lane_ok * row_ok
        for j in range(4):
            x_r = pr[j, pl.ds(r, 8), :]
            x_l = pl_[j, pl.ds(r, 8), :]
            for s in range(SLOTS):
                q = SLOTS * j + s
                x = jnp.where(right_lane, roll(x_r, -W * s), jnp.where(left_lane, roll(x_l, -W - W * s), 0.0))
                if q < CZ:
                    vb[0, 1 + q, pl.ds(r, 8), :] = x * ok
                elif q < 2 * CZ:
                    sb[q - CZ, pl.ds(r, 8), :] = x
                elif q < 2 * CZ + 4:
                    cb[q - 2 * CZ, pl.ds(r, 8), :] = x
                else:
                    wb[q - 2 * CZ - 4, pl.ds(r, 8), :] = x * ok
        return carry

    lax.fori_loop(0, (HI - LO) // 8, unpack, 0)

    def mask_rows(l, carry):
        va[0, l, LO:OFF] = va[0, l, LO:OFF] * top_ok
        va[0, l, OFF + BR : HI] = va[0, l, OFF + BR : HI] * bot_ok
        return carry

    lax.fori_loop(1, CZ + 1, mask_rows, 0)
    for k in range(4):
        wa[k, NLO:OFF] = wa[k, NLO:OFF] * top_ok
        wa[k, OFF + BR : NHI] = wa[k, OFF + BR : NHI] * bot_ok
        ca[k, NLO:NHI] = ci[k, NLO:NHI].astype(F32)

    step = 16
    lane16 = lanes((step, BC))
    first, last = lane16 == 0, lane16 == BC - 1
    lane_ok16 = jnp.where(lane16 < BC // 2, right_ok, left_ok)

    def row_ok_of(r):
        return top_ok if r < OFF else bot_ok if r >= OFF + BR else None

    def segments(lo, hi):
        return chunks(lo, OFF, step) + chunks(OFF, OFF + BR, step) + chunks(OFF + BR, hi, step)

    def fold(x):
        return jnp.sum(x.reshape(x.shape[0] // 8, 8, BC), axis=0)

    def apply(sa_ref, sb_ref, k, da_ref, db_ref, kd, lo, hi, beside=True):
        def layer(l, acc):
            acc0, acc1 = acc
            for r, n in segments(lo, hi):
                rows = slice(r, r + n)
                a, b = sa_ref[k, l, rows], sb_ref[k, l, rows]
                f, e = first[:n], last[:n]
                near = roll(jnp.where(e, b, a), 1) + roll(jnp.where(f, b, a), -1)
                near = near + (sa_ref[k, l, r - 1 : r - 1 + n] + sa_ref[k, l, r + 1 : r + 1 + n])
                near = near + (sa_ref[k, l - 1, rows] + sa_ref[k, l + 1, rows])
                out = sa[l - 1, rows] * a - near
                ok = row_ok_of(r)
                if ok is not None:
                    out = out * ok
                else:
                    acc0 = acc0 + fold(a * a)
                    acc1 = acc1 + fold(a * out)
                if da_ref is not None:
                    da_ref[kd, l, rows] = out
                if beside:
                    near = roll(jnp.where(e, a, b), 1) + roll(jnp.where(f, a, b), -1)
                    near = near + (sb_ref[k, l, r - 1 : r - 1 + n] + sb_ref[k, l, r + 1 : r + 1 + n])
                    near = near + (sb_ref[k, l - 1, rows] + sb_ref[k, l + 1, rows])
                    out = sb[l - 1, rows] * b - near
                    okb = lane_ok16[:n] if ok is None else lane_ok16[:n] * ok
                    db_ref[kd, l, rows] = out * okb
            return acc0, acc1

        z = jnp.zeros((8, BC), F32)
        return lax.fori_loop(1, CZ + 1, layer, (z, z))

    row_lane = lanes((1, BC))

    def send_sums(n, accs):
        row = jnp.zeros((1, BC), F32)
        for k, acc in enumerate(accs):
            row = row + jnp.where(row_lane == k, jnp.sum(acc, keepdims=True), 0.0)
        mrow[n, 0] = row
        mbuf[n, me] = row

        def go(o, carry):
            pltpu.make_async_remote_copy(
                mrow.at[n, 0], mbuf.at[n, me], as_.at[n], ar.at[n], device_id=peer(o), device_id_type=MESH
            ).start()
            return carry

        lax.fori_loop(1, NPEER, go, 0)

    def others(n):
        return mbuf.at[n, pl.ds(0, NPEER - 1)]

    def total_sums(n):
        pltpu.make_async_copy(others(n), others(n), ar.at[n]).wait()
        total = jnp.sum(mbuf[n], axis=0)
        mz[n, 2] = total
        for side, dev in ((0, above), (1, below)):
            pltpu.make_async_remote_copy(
                mz.at[n, 2], mz.at[n, side], zs.at[n, side], zr.at[n, side],
                device_id=(dev, gx, gy), device_id_type=MESH,
            ).start()
        return total

    def wait_z(n):
        for side, dev in ((0, above), (1, below)):
            pltpu.make_async_remote_copy(
                mz.at[n, 2], mz.at[n, side], zs.at[n, side], zr.at[n, side],
                device_id=(dev, gx, gy), device_id_type=MESH,
            ).wait()

    def coefficients(total):
        m = [jnp.sum(jnp.where(row_lane == k, total, 0.0), axis=1, keepdims=True) for k in range(6)]
        h = [m[k + 1] + SHIFT * m[k] for k in range(5)]
        l10, l20 = h[1] / h[0], h[2] / h[0]
        d1 = h[2] - l10 * h[1]
        e12 = h[3] - l20 * h[1]
        l21 = e12 / d1
        d2 = h[4] - l20 * h[2] - l21 * e12
        y1 = m[1] - l10 * m[0]
        y2 = m[2] - l20 * m[0] - l21 * y1
        c2 = y2 / d2
        c1 = y1 / d1 - l21 * c2
        c0 = m[0] / h[0] - l10 * c1 - l20 * c2
        return [jnp.broadcast_to(c, (step, BC)) for c in (c0, c1, c2)]

    fsends = []

    def send_faces(n, a_ref, b_ref, dn, up, sem_s, sem_r):
        out = []
        for side, (l, dst, dev) in enumerate(((1, dn, below), (CZ, up, above))):
            for r, cnt in chunks(NLO, NHI, step):
                lane = lane16[:cnt]
                x = b_ref[0, l, r : r + cnt]
                for k in (1, 2):
                    mine = (lane >= 2 * W * k - W) & (lane < 2 * W * k + W)
                    x = jnp.where(mine, roll(b_ref[k, l, r : r + cnt], 2 * W * k), x)
                stage[n, side, r - NLO : r - NLO + cnt] = x
            for k in range(4):
                src = stage.at[n, side] if k == 3 else a_ref.at[k, l, pl.ds(NLO, NHI - NLO), :]
                c = pltpu.make_async_remote_copy(
                    src, dst.at[k], sem_s.at[4 * side + k], sem_r.at[4 * side + k],
                    device_id=(dev, gx, gy), device_id_type=MESH,
                )
                c.start()
                out.append(c)
        return out

    def received(ref, c, r, n):
        at = slice(r - NLO, r - NLO + n)
        x = [c[k][:n] * ref[k, at] for k in range(3)]
        packed = ref[3, at]
        y = [c[k][:n] * roll(packed, -2 * W * k) for k in range(3)]
        return x[0] + x[1] + x[2], y[0] + y[1] + y[2]

    def pull(lo, hi, beside):
        for r, n in chunks(lo - 8, hi + 8, step):
            a, b = fa[r : r + n], fb[r : r + n]
            for d in range(SPAN):
                x, y = moved(a, b, d - REACH)
                sha[d, r : r + n] = x
                if beside:
                    shb[d, r : r + n] = y
        for r, n in chunks(lo, hi, step):
            x = y = jnp.zeros((n, BC), F32)
            for c in range(SPAN * SPAN):
                dx, d = c // SPAN - REACH, c % SPAN
                x = x + ta[c, r : r + n] * sha[d, r + dx : r + dx + n]
                if beside:
                    y = y + tb[c, r : r + n] * shb[d, r + dx : r + dx + n]
            yield r, n, x, y

    def push(lo, hi, beside):
        for r, n in chunks(lo, hi, step):
            x = y = jnp.zeros((n, BC), F32)
            for d in range(SPAN):
                p = q = jnp.zeros((n, BC), F32)
                for dx in range(-REACH, REACH + 1):
                    c = (dx + REACH) * SPAN + d
                    p = p + ta[c, r - dx : r - dx + n] * ma[r - dx : r - dx + n]
                    q = q + tb[c, r - dx : r - dx + n] * mb[r - dx : r - dx + n]
                p, q = moved(p, q, REACH - d)
                x, y = x + p, y + q
            if beside:
                ok = lane_ok16[:n]
                row_ok = row_ok_of(r) if n == 8 else None
                if row_ok is not None:
                    x, ok = x * row_ok, ok * row_ok
                y = y * ok
            yield r, n, x, y

    s01 = apply(va, vb, 0, va, vb, 1, LO, HI)
    s23 = apply(va, vb, 1, va, vb, 2, LO, HI)
    faces = send_faces(0, va, vb, fdn, fup, fs, fr)
    s45 = apply(va, vb, 2, va, vb, 3, NLO, NHI)
    send_sums(0, s01 + s23 + s45)

    def tables(c, carry):
        code_at = c.astype(F32)
        for r, n in chunks(NLO, NHI, step):
            rows = slice(r, r + n)
            x = y = jnp.zeros((n, BC), F32)
            for k in range(4):
                x = x + jnp.where(ca[k, rows] == code_at, wa[k, rows], 0.0)
                y = y + jnp.where(cb[k, rows] == code_at, wb[k, rows], 0.0)
            ta[c, rows] = x
            tb[c, rows] = y
        return carry

    lax.fori_loop(0, SPAN * SPAN, tables, 0)

    co = coefficients(total_sums(0))
    g = [1.0 - SHIFT * co[0], -(co[0] + SHIFT * co[1]), -(co[1] + SHIFT * co[2]), -co[2]]

    def residual(l, carry):
        for r, n in chunks(NLO, NHI, step):
            rows = slice(r, r + n)
            ua[0, l, rows] = (g[0][:n] * va[0, l, rows] + g[1][:n] * va[1, l, rows]) + (
                g[2][:n] * va[2, l, rows] + g[3][:n] * va[3, l, rows]
            )
            ub[0, l, rows] = (g[0][:n] * vb[0, l, rows] + g[1][:n] * vb[1, l, rows]) + (
                g[2][:n] * vb[2, l, rows] + g[3][:n] * vb[3, l, rows]
            )
        return carry

    lax.fori_loop(1, CZ + 1, residual, 0)

    wait_z(0)
    for c in faces:
        c.wait()
    cm, cp = coefficients(mz[0, 0]), coefficients(mz[0, 1])

    def combine(refs, k3, l, rows, n):
        a = refs[0]
        return (k3[0][:n] * a[0, l, rows] + k3[1][:n] * a[1, l, rows]) + k3[2][:n] * a[2, l, rows]

    for r, n in chunks(LO, HI, step):
        rows = slice(r, r + n)
        fa[rows] = combine((va,), co, CZ, rows, n)
        fb[rows] = combine((vb,), co, CZ, rows, n)
    scale_up = RATE * up_ok
    for r, n, x, y in pull(NLO, NHI, True):
        p, q = received(fdn, cp, r, n)
        ma[r : r + n] = scale_up * (p - x)
        mb[r : r + n] = scale_up * (q - y)
    for edge in (LO, NHI):
        ma[edge : edge + 8] = z8
        mb[edge : edge + 8] = z8
    for r0, r1 in ((NLO, OFF), (OFF, OFF + BR), (OFF + BR, NHI)):
        for r, n, x, y in push(r0, r1, True):
            ua[0, CZ, r : r + n] = ua[0, CZ, r : r + n] + x
            ub[0, CZ, r : r + n] = ub[0, CZ, r : r + n] + y

    for r, n in chunks(NLO, NHI, step):
        x, y = received(fup, cm, r, n)
        fa[r : r + n] = x
        fb[r : r + n] = y
    scale_dn = RATE * dn_ok
    for edge in (LO, NHI):
        fa[edge : edge + 8] = z8
        fb[edge : edge + 8] = z8
    low = []
    for r, n, x, y in pull(NLO, NHI, True):
        rows = slice(r, r + n)
        x = scale_dn * (combine((va,), co, 1, rows, n) - x)
        y = scale_dn * (combine((vb,), co, 1, rows, n) - y)
        ua[0, 1, rows] = ua[0, 1, rows] - x
        ub[0, 1, rows] = ub[0, 1, rows] - y
        stage[0, 2, r - NLO : r - NLO + n] = x

    t01 = apply(ua, ub, 0, ua, ub, 1, NLO, NHI)
    t23 = apply(ua, ub, 1, ua, ub, 2, NLO, NHI)
    faces = send_faces(1, ua, ub, gdn, gup, gs, gr)
    t45 = apply(ua, ub, 2, None, None, 0, OFF, OFF + BR, beside=False)
    send_sums(1, t01 + t23 + t45)

    zc = jnp.zeros((step, BC), F32)

    def clear(l, carry):
        for r, n in chunks(0, BR, step):
            ifl[l, r : r + n] = zc
        return carry

    lax.fori_loop(1, CZ - 1, clear, 0)

    eo = coefficients(total_sums(1))

    def answer(l, carry):
        for r, n in chunks(OFF, OFF + BR, step):
            rows = slice(r, r + n)
            x = combine((va,), co, l, rows, n) + combine((ua,), eo, l, rows, n)
            sol[l - 1, r - OFF : r - OFF + n] = x
        return carry

    lax.fori_loop(1, CZ + 1, answer, 0)

    wait_z(1)
    for c in faces:
        c.wait()
    em, ep = coefficients(mz[1, 0]), coefficients(mz[1, 1])

    for r, n in chunks(NLO, NHI, step):
        rows = slice(r, r + n)
        fa[rows] = combine((ua,), eo, CZ, rows, n)
        fb[rows] = combine((ub,), eo, CZ, rows, n)
    for r, n, x, y in pull(NLO, NHI, True):
        p, q = received(gdn, ep, r, n)
        ma[r : r + n] = 2.0 * ma[r : r + n] + scale_up * (p - x)
        mb[r : r + n] = 2.0 * mb[r : r + n] + scale_up * (q - y)
    for r, n, x, y in push(OFF, OFF + BR, False):
        ifl[CZ - 1, r - OFF : r - OFF + n] = x

    for r, n in chunks(NLO, NHI, step):
        x, y = received(gup, em, r, n)
        fa[r : r + n] = x
        fb[r : r + n] = y
    for r, n, x, y in pull(OFF, OFF + BR, False):
        rows = slice(r, r + n)
        x = 2.0 * stage[0, 2, r - NLO : r - NLO + n] + scale_dn * (combine((ua,), eo, 1, rows, n) - x)
        ifl[0, r - OFF : r - OFF + n] = -x

    for c in sends:
        c.wait_send()
    for n in range(2):
        pltpu.make_async_copy(others(n), others(n), as_.at[n]).wait()


def per_device(load, stiffness, pair_code, pair_weight):
    field = lambda k: pltpu.VMEM((k, CZ + 2, ROWS, BC), F32)
    plane = lambda *lead: pltpu.VMEM((*lead, ROWS, BC), F32)
    near = lambda *lead: pltpu.VMEM((*lead, NHI - NLO, BC), F32)
    dma = pltpu.SemaphoreType.DMA
    nsend = 22
    scratch = [
        field(4), field(4), field(3), field(3), plane(CZ), plane(CZ),
        pltpu.VMEM((4, ROWS, BC), jnp.int32), plane(4), plane(4), plane(4), plane(4),
        pltpu.VMEM((4, BR, BC), F32), pltpu.VMEM((4, BR, BC), F32), plane(4), plane(4),
        plane(SPAN * SPAN), plane(SPAN * SPAN), plane(SPAN), plane(SPAN), plane(), plane(), plane(), plane(),
        near(2, 3), near(4), near(4), near(4), near(4),
        pltpu.VMEM((2, 1, 1, BC), F32), pltpu.VMEM((2, NPEER, 1, BC), F32), pltpu.VMEM((2, 3, 1, BC), F32),
        dma((4,)), dma((nsend,)), dma((nsend,)), dma((8,)), dma((8,)), dma((8,)), dma((8,)),
        dma((2,)), dma((2,)), dma((2, 2)), dma((2, 2)),
    ]
    out = jax.ShapeDtypeStruct((CZ, BR, BC), F32)
    return pl.pallas_call(
        kernel,
        out_shape=(out, out),
        in_specs=[pl.BlockSpec(memory_space=pl.ANY)] * 4,
        out_specs=[pl.BlockSpec(memory_space=pltpu.VMEM)] * 2,
        scratch_shapes=scratch,
        compiler_params=pltpu.CompilerParams(collective_id=0, has_side_effects=True),
        name="uzawa",
    )(load, stiffness, pair_code, pair_weight)


def solution(mesh):
    return jax.shard_map(
        per_device,
        mesh=mesh,
        in_specs=(
            P("body", "gx", "gy"),
            P("body", "gx", "gy"),
            P(None, "gx", "gy"),
            P(None, "gx", "gy"),
        ),
        out_specs=(P("body", "gx", "gy"), P("body", "gx", "gy")),
        check_vma=False,
    )
```

time: 346 us -> 53.3 us (0.15); the launches traced: 342 us -> 53.2 us
  starting transfers between devices: 165 us -> 0 us
  Pallas kernels: 0 us -> 49.8 us
  blocking collectives: 46.8 us -> 0 us
  other arithmetic: 40.8 us -> 0 us
  waiting for transfers between devices: 37.4 us -> 0 us
  local copies, waits for them, and re-layouts: 29.4 us -> 2.74 us
  between operations: 22.1 us -> 0.65 us
    ppermute x52 -> x0, starting transfers between devices: 142 us -> none  [the longest x24 84.5 us: with_halo(): lax.ppermute(tail, axis, [(i, (i + 1) % count) for i in range(ends)])]
    pallas_call x0 -> x1, Pallas kernels: none -> 49.8 us  [per_device(): pl.pallas_call(kernel, out_shape=(out, out), in_specs=[pl.BlockSpec(memor...]
    all_to_all x3 -> x0, blocking collectives: 46.8 us -> none  [sent_to_all(): return lax.all_to_all(copies, axis, split_axis=0, concat_axis=0, tiled=True)]
    ppermute x52 -> x0, waiting for transfers between devices: 29.2 us -> none  [the longest x24 14.8 us: with_halo(): lax.ppermute(head, axis, [((i + 1) % count, i) for i in range(ends)])]
    all_to_all x3 -> x0, starting transfers between devices: 22.9 us -> none  [sent_to_all(): return lax.all_to_all(copies, axis, split_axis=0, concat_axis=0, tiled=True)]
    concatenate x28 -> x0, other arithmetic: 18.9 us -> none  [the longest x22 10.8 us: with_halo(): jnp.concatenate([lax.ppermute(tail, axis, [(i, (i + 1) % count) for i in...]
    slice x47 -> x0, local copies, waits for them, and re-layouts: 18.7 us -> none  [the longest x16 9.8 us: with_halo(): head = lax.slice_in_dim(cells, 0, width, axis=dim)]
    reduce_sum x13 -> x0, other arithmetic: 13.9 us -> none  [the longest x6 10.3 us: two_products(): jnp.sum(residual * residual)]
  transfers between devices with their start and end apart: 55 -> 0, of which waited for: 21 -> 0; matrix products, arithmetic and copies ran while one was open for 9% -> 0% of each run, Pallas kernels for 0% -> 0%
where the time goes in v1:
time: 53.3 us; the launch traced here: 53.2 us
  Pallas kernels  49.8 us (93%)
  local copies, waits for them, and re-layouts  2.74 us (5%)
  between operations  0.65 us (1%)
    pallas_call x1, Pallas kernels, per_device(): pl.pallas_call(kernel, out_shape=(out, out), in_specs=[pl.BlockSpec(memor...  49.8 us
    unnamed x4, local copies, waits for them, and re-layouts  2.74 us

profile of v1, /device:TPU:1, one launch (start us, length us, event | category | flops | bytes accessed | tf_op | source)
XLA Modules:
  0.0 53.2 jit_solution(16772555588972210359)
XLA Ops:
  0.6 49.8 %uzawa.1 = (f32[16,64,128]{2,1,0:T(8,128)}, f32[16,64,128]{2,1,0:T(8,128)}) custom-call(f32[16,64,128]{2,1,0:T(8,128)} %load.1, f32[16,64,128]{2,1,0:T(8,128)} %stiff.1, s32[4,64,128]{2,1,0:T(8,128)} %code.1, f32[4,64,128]{2,1,0:T(8,128)} %weight.1), custom_call_target="tpu_custom_call" | custom-call | tf_op jit(solution)/shard_map/uzawa/pallas_call | solution.py:529
  50.4 0.0 copy-start
  50.5 1.9 %copy.8 = f32[16,64,128]{2,1,0:T(8,128)} copy(f32[16,64,128]{2,1,0:T(8,128)} %get-tuple-element.4) | data formatting | bytes 1048576
  52.4 0.0 copy-done
  52.4 0.8 %copy.9 = f32[16,64,128]{2,1,0:T(8,128)} copy(f32[16,64,128]{2,1,0:T(8,128)S(1)} %copy-done) | data formatting | bytes 1048576
Async XLA Ops:
  50.4 2.0 %copy-start = (f32[16,64,128]{2,1,0:T(8,128)S(1)}, f32[16,64,128]{2,1,0:T(8,128)}, u32[]{:S(2)}) copy-start(f32[16,64,128]{2,1,0:T(8,128)} %get-tuple-element.5) | copy-start | bytes 1572868
